TPU v7x, 32 devices: a whole 2x2x4 slice. The times are simulated.
32 devices in a mesh: fsdp: 4 (over x, core), ctx: 2 (over y), tp: 4 (over z).
Axes of the slice: x: 2, y: 2, z: 4, core: 2. Of those that a mesh axis runs over, the one named last changes fastest.
Arguments:
- tokens: bfloat16 [8, 1024, 768], P('fsdp', 'ctx'), may hold values from -6 to 6
- segments: int32 [8, 1024], P('fsdp', 'ctx'), may hold values from 0 to 3, never falling along the last dimension, each value on 1 to 768 neighbouring positions
- ln_gains: bfloat16 [2, 768], P(None, 'fsdp'), may hold values from 0.5 to 1.5
- ln_biases: bfloat16 [2, 768], P(None, 'fsdp'), may hold values from -1.75 to 1.75
- w_qkv: bfloat16 [3, 768, 768], P(None, 'fsdp', 'tp'), may hold values from -0.21875 to 0.21875
- bias_qv: bfloat16 [2, 12, 64], P(None, 'tp', 'fsdp'), may hold values from -3 to 3
- w_out: bfloat16 [768, 768], P('tp', 'fsdp'), may hold values from -1.25 to 1.25
- out_biases: bfloat16 [2, 768], P(None, 'fsdp'), may hold values from -1.75 to 1.75
- w_up: bfloat16 [768, 3072], P('fsdp', 'tp'), may hold values from -0.21875 to 0.21875
- up_bias: bfloat16 [48, 64], P('tp', 'fsdp'), may hold values from -3 to 3
- w_down: bfloat16 [3072, 768], P('tp', 'fsdp'), may hold values from -0.109375 to 0.109375
- cotangent: bfloat16 [8, 1024, 768], P('fsdp', 'ctx'), may hold values from -6 to 6
Outputs:
- output: bfloat16 [8, 1024, 768], P('fsdp', 'ctx')
- grad_tokens: float32 [8, 1024, 768], P('fsdp', 'ctx')
- grad_ln_gains: float32 [2, 768], P(None, 'fsdp')
- grad_ln_biases: float32 [2, 768], P(None, 'fsdp')
- grad_qkv: float32 [3, 768, 768], P(None, 'fsdp', 'tp')
- grad_bias_qv: float32 [2, 12, 64], P(None, 'tp', 'fsdp')
- grad_out_proj: float32 [768, 768], P('tp', 'fsdp')
- grad_out_biases: float32 [2, 768], P(None, 'fsdp')
- grad_up: float32 [768, 3072], P('fsdp', 'tp')
- grad_up_bias: float32 [48, 64], P('tp', 'fsdp')
- grad_down: float32 [3072, 768], P('tp', 'fsdp')
Inputs may be any that keep to these rules, and one draw needn't show every extreme that they name: `segments`: within each sequence the numbers never fall; each document holds 1 to 768 positions, and one document of each sequence exactly that many.
All inputs are finite; a program needn't handle non-finite values.
Results may differ from a plain program's by a relative error of at most 0.017.
Values may be sent and summed in bfloat16 or wider, within the bound.
No kernel may reach another device: no remote copies, remote signals or barrier semaphores. Data moves between devices by JAX's collectives and lax.ppermute only.
A program may use at most 384 MiB of HBM per device.

v0:
```python
import jax
import jax.numpy as jnp
from jax import lax
from jax.sharding import PartitionSpec as P

HD = 64


eps = 1e-05
masked_score = -1e30


def layer_norm(values_in, gain, shift):
    average = jnp.mean(values_in, axis=-1, keepdims=True)
    centered = values_in - average
    variance = jnp.mean(centered * centered, axis=-1, keepdims=True)
    return centered * lax.rsqrt(variance + eps) * gain + shift


def gelu_tanh(values_in):
    return jax.nn.gelu(values_in, approximate=True)


def block_scores(queries, key_rows, query_place, query_doc, key_place, key_doc):
    scores = (
        jnp.einsum("qhd,khd->hqk", queries, key_rows, preferred_element_type=jnp.float32) * 0.125
    )
    allowed = (query_doc[:, None] == key_doc[None, :]) & (
        key_place[None, :] <= query_place[:, None]
    )
    return jnp.where(allowed[None], scores, masked_score)


def tp_total(make, row_count):
    return lax.psum(make(0, row_count), "tp")


def local(
    tokens,
    segments,
    ln_gains,
    ln_biases,
    w_qkv,
    bias_qv,
    w_out,
    out_biases,
    w_up,
    up_bias,
    w_down,
    cotangent,
):
    gathered = (
        lax.all_gather(ln_gains, "fsdp", axis=1, tiled=True),
        lax.all_gather(ln_biases, "fsdp", axis=1, tiled=True),
        lax.all_gather(w_qkv, "fsdp", axis=1, tiled=True),
        lax.all_gather(bias_qv, "fsdp", axis=2, tiled=True),
        lax.all_gather(w_out, "fsdp", axis=1, tiled=True),
        lax.all_gather(out_biases, "fsdp", axis=1, tiled=True),
        lax.all_gather(w_up, "fsdp", axis=0, tiled=True),
        lax.all_gather(up_bias, "fsdp", axis=1, tiled=True),
        lax.all_gather(w_down, "fsdp", axis=1, tiled=True),
    )
    (
        gain_rows,
        shift_rows,
        qkv_proj,
        qv_bias,
        out_proj,
        branch_bias,
        up_proj,
        up_shift,
        down_proj,
    ) = gathered
    gain_rows = gain_rows.astype(jnp.float32)
    shift_rows = shift_rows.astype(jnp.float32)
    branch_bias = branch_bias.astype(jnp.float32)
    seq_count, block_len, width = tokens.shape
    row_count = seq_count * block_len
    width_heads = qkv_proj.shape[2]
    head_count = width_heads // HD
    inputs = tokens.astype(jnp.float32).reshape(row_count, width)
    cot_rows = cotangent.reshape(row_count, width)
    normed_low = layer_norm(inputs, gain_rows[0], shift_rows[0]).astype(jnp.bfloat16)
    projected = jnp.einsum("td,cdh->cth", normed_low, qkv_proj, preferred_element_type=jnp.float32)
    bias_flat = qv_bias.astype(jnp.float32).reshape(2, width_heads)
    query_low = (projected[0] + bias_flat[0]).astype(jnp.bfloat16)
    key_low = projected[1].astype(jnp.bfloat16)
    value_low = (projected[2] + bias_flat[1]).astype(jnp.bfloat16)
    pair_local = jnp.concatenate([key_low, value_low], axis=1).reshape(
        seq_count, block_len, 2 * width_heads
    )
    pair_rows, doc_rows = (
        lax.all_gather(pair_local, "ctx", axis=1, tiled=True),
        lax.all_gather(segments.astype(jnp.bfloat16), "ctx", axis=1, tiled=True),
    )
    full_len = pair_rows.shape[1]
    key_rows = pair_rows[:, :, :width_heads].reshape(seq_count, full_len, head_count, HD)
    value_rows = pair_rows[:, :, width_heads:].reshape(seq_count, full_len, head_count, HD)
    key_doc = doc_rows.astype(jnp.float32)
    key_place = jnp.arange(full_len, dtype=jnp.int32)
    block_rows = min(512, block_len)
    block_count = block_len // block_rows
    query_place = (
        lax.axis_index("ctx") * block_len + jnp.arange(block_len, dtype=jnp.int32)
    ).reshape(block_count, block_rows)
    query_doc = segments.astype(jnp.float32).reshape(seq_count, block_count, block_rows)
    query_blocks = query_low.reshape(seq_count, block_count, block_rows, head_count, HD)

    def forward_sequence(seq_item):
        seq_queries, seq_keys, seq_values, seq_key_doc, seq_query_doc = seq_item

        def forward_block(block_item):
            queries, places, doc_ids = block_item
            scores = block_scores(queries, seq_keys, places, doc_ids, key_place, seq_key_doc)
            row_max = jnp.max(scores, axis=-1, keepdims=True)
            exponent = jnp.exp(scores - row_max)
            totals = jnp.sum(exponent, axis=-1, keepdims=True)
            probability = (exponent / totals).astype(jnp.bfloat16)
            mixture = jnp.einsum(
                "hqk,khd->qhd", probability, seq_values, preferred_element_type=jnp.float32
            )
            return (mixture, (row_max + jnp.log(totals))[..., 0])

        return lax.map(forward_block, (seq_queries, query_place, seq_query_doc))

    mixture, log_sums = lax.map(
        forward_sequence, (query_blocks, key_rows, value_rows, key_doc, query_doc)
    )
    attended_low = mixture.reshape(row_count, width_heads).astype(jnp.bfloat16)

    def make_attn(start, count):
        return jnp.dot(attended_low, out_proj, preferred_element_type=jnp.float32)

    branch_part = tp_total(make_attn, row_count)
    hidden = inputs + branch_part + branch_bias[0]
    normed_two, norm_two_pull = jax.vjp(layer_norm, hidden, gain_rows[1], shift_rows[1])
    normed_two_own = normed_two.astype(jnp.bfloat16)
    pre_act = jnp.dot(
        normed_two_own, up_proj, preferred_element_type=jnp.float32
    ) + up_shift.astype(jnp.float32).reshape(-1)
    activated, gelu_pull = jax.vjp(gelu_tanh, pre_act)
    activated_low = activated.astype(jnp.bfloat16)

    def make_down(start, count):
        return jnp.dot(activated_low, down_proj, preferred_element_type=jnp.float32)

    second = tp_total(make_down, row_count) + branch_bias[1]
    result_own = (hidden + second).astype(jnp.bfloat16)
    qkv_back, out_back, up_back, down_back = (
        lax.all_gather(w_qkv, "fsdp", axis=1, tiled=True),
        lax.all_gather(w_out, "fsdp", axis=1, tiled=True),
        lax.all_gather(w_up, "fsdp", axis=0, tiled=True),
        lax.all_gather(w_down, "fsdp", axis=1, tiled=True),
    )
    grad_act_low = jnp.einsum(
        "td,fd->tf", cot_rows, down_back, preferred_element_type=jnp.float32
    ).astype(jnp.bfloat16)
    (grad_pre,) = gelu_pull(grad_act_low.astype(jnp.float32))
    grad_pre_low = grad_pre.astype(jnp.bfloat16)
    grad_down = jnp.einsum("tf,td->fd", activated_low, cot_rows, preferred_element_type=jnp.float32)
    grad_up = jnp.einsum(
        "td,tf->df", normed_two_own, grad_pre_low, preferred_element_type=jnp.float32
    )
    grad_up_bias = jnp.sum(grad_pre_low.astype(jnp.float32), axis=0).reshape(up_shift.shape)

    def make_mlp_back(start, count):
        return jnp.einsum("tf,df->td", grad_pre_low, up_back, preferred_element_type=jnp.float32)

    grad_normed_two = tp_total(make_mlp_back, row_count)
    grad_hidden_norm, grad_gain_two, grad_shift_two = norm_two_pull(grad_normed_two)
    grad_hidden = cot_rows.astype(jnp.float32) + grad_hidden_norm
    grad_branch_own = grad_hidden.astype(jnp.bfloat16)
    grad_out_proj = jnp.einsum(
        "th,td->hd", attended_low, grad_branch_own, preferred_element_type=jnp.float32
    )
    grad_attended = jnp.einsum(
        "td,hd->th", grad_branch_own, out_back, preferred_element_type=jnp.float32
    ).astype(jnp.bfloat16)
    grad_blocks = grad_attended.reshape(seq_count, block_count, block_rows, head_count, HD)

    def backward_sequence(seq_item):
        seq_queries, seq_grads, seq_logs, seq_keys, seq_values, seq_key_doc, seq_query_doc = (
            seq_item
        )

        def backward_block(running, block_item):
            key_sum, value_sum = running
            queries, grad_rows, log_sum, places, doc_ids = block_item
            scores = block_scores(queries, seq_keys, places, doc_ids, key_place, seq_key_doc)
            probability = jnp.exp(scores - log_sum[..., None])
            grad_prob = jnp.einsum(
                "qhd,khd->hqk", grad_rows, seq_values, preferred_element_type=jnp.float32
            )
            inner_sum = jnp.sum(probability * grad_prob, axis=-1, keepdims=True)
            grad_scores = (probability * (grad_prob - inner_sum) * 0.125).astype(jnp.bfloat16)
            grad_query = jnp.einsum(
                "hqk,khd->qhd", grad_scores, seq_keys, preferred_element_type=jnp.float32
            )
            key_sum = key_sum + jnp.einsum(
                "hqk,qhd->khd", grad_scores, queries, preferred_element_type=jnp.float32
            )
            value_sum = value_sum + jnp.einsum(
                "hqk,qhd->khd",
                probability.astype(jnp.bfloat16),
                grad_rows,
                preferred_element_type=jnp.float32,
            )
            return ((key_sum, value_sum), grad_query)

        zero_rows = jnp.zeros((full_len, head_count, HD), jnp.float32)
        (key_sum, value_sum), grad_query = lax.scan(
            backward_block,
            (zero_rows, zero_rows),
            (seq_queries, seq_grads, seq_logs, query_place, seq_query_doc),
        )
        return (key_sum, value_sum, grad_query)

    key_sum, value_sum, grad_query = lax.map(
        backward_sequence,
        (query_blocks, grad_blocks, log_sums, key_rows, value_rows, key_doc, query_doc),
    )
    pair_terms = jnp.concatenate(
        [
            key_sum.reshape(seq_count, full_len, width_heads),
            value_sum.reshape(seq_count, full_len, width_heads),
        ],
        axis=2,
    )
    pair_low = lax.psum_scatter(
        pair_terms.astype(jnp.bfloat16), "ctx", scatter_dimension=1, tiled=True
    ).reshape(row_count, 2 * width_heads)
    query_grad_low = grad_query.reshape(row_count, width_heads).astype(jnp.bfloat16)
    grad_proj_low = jnp.stack(
        [query_grad_low, pair_low[:, :width_heads], pair_low[:, width_heads:]]
    )
    grad_qkv = jnp.einsum(
        "td,cth->cdh", normed_low, grad_proj_low, preferred_element_type=jnp.float32
    )
    grad_qv_bias = jnp.stack(
        [
            jnp.sum(query_grad_low.astype(jnp.float32), axis=0),
            jnp.sum(pair_low[:, width_heads:].astype(jnp.float32), axis=0),
        ]
    ).reshape(qv_bias.shape)

    def make_qkv_back(start, count):
        return jnp.einsum(
            "cth,cdh->td", grad_proj_low, qkv_back, preferred_element_type=jnp.float32
        )

    grad_normed = tp_total(make_qkv_back, row_count)
    first_norm, first_pull = jax.vjp(layer_norm, inputs, gain_rows[0], shift_rows[0])
    grad_input_norm, grad_gain_one, grad_shift_one = first_pull(grad_normed)
    grad_tokens_own = grad_hidden + grad_input_norm
    norm_grads = jnp.stack([grad_gain_one, grad_gain_two, grad_shift_one, grad_shift_two])
    grad_gains = norm_grads[0:2]
    grad_shifts = norm_grads[2:4]
    grad_biases = jnp.stack(
        [
            jnp.sum(grad_branch_own.astype(jnp.float32), axis=0),
            jnp.sum(cot_rows.astype(jnp.float32), axis=0),
        ]
    )
    (
        part_gains,
        part_shifts,
        part_qkv,
        part_qv,
        part_out,
        part_biases,
        part_up,
        part_upb,
        part_down,
    ) = (
        lax.psum_scatter(
            grad_gains.astype(jnp.bfloat16), "fsdp", scatter_dimension=1, tiled=True
        ).astype(jnp.float32),
        lax.psum_scatter(
            grad_shifts.astype(jnp.bfloat16), "fsdp", scatter_dimension=1, tiled=True
        ).astype(jnp.float32),
        lax.psum_scatter(
            grad_qkv.astype(jnp.bfloat16), "fsdp", scatter_dimension=1, tiled=True
        ).astype(jnp.float32),
        lax.psum_scatter(
            grad_qv_bias.astype(jnp.bfloat16), "fsdp", scatter_dimension=2, tiled=True
        ).astype(jnp.float32),
        lax.psum_scatter(
            grad_out_proj.astype(jnp.bfloat16), "fsdp", scatter_dimension=1, tiled=True
        ).astype(jnp.float32),
        lax.psum_scatter(
            grad_biases.astype(jnp.bfloat16), "fsdp", scatter_dimension=1, tiled=True
        ).astype(jnp.float32),
        lax.psum_scatter(
            grad_up.astype(jnp.bfloat16), "fsdp", scatter_dimension=0, tiled=True
        ).astype(jnp.float32),
        lax.psum_scatter(
            grad_up_bias.astype(jnp.bfloat16), "fsdp", scatter_dimension=1, tiled=True
        ).astype(jnp.float32),
        lax.psum_scatter(
            grad_down.astype(jnp.bfloat16), "fsdp", scatter_dimension=1, tiled=True
        ).astype(jnp.float32),
    )
    reduced = (
        lax.psum(part_gains.astype(jnp.bfloat16), "ctx").astype(jnp.float32),
        lax.psum(part_shifts.astype(jnp.bfloat16), "ctx").astype(jnp.float32),
        lax.psum(part_qkv.astype(jnp.bfloat16), "ctx").astype(jnp.float32),
        lax.psum(part_qv.astype(jnp.bfloat16), "ctx").astype(jnp.float32),
        lax.psum(part_out.astype(jnp.bfloat16), "ctx").astype(jnp.float32),
        lax.psum(part_biases.astype(jnp.bfloat16), "ctx").astype(jnp.float32),
        lax.psum(part_up.astype(jnp.bfloat16), "ctx").astype(jnp.float32),
        lax.psum(part_upb.astype(jnp.bfloat16), "ctx").astype(jnp.float32),
        lax.psum(part_down.astype(jnp.bfloat16), "ctx").astype(jnp.float32),
    )
    result = result_own.reshape(seq_count, block_len, width)
    grad_tokens = grad_tokens_own.reshape(seq_count, block_len, width)
    return (
        result,
        grad_tokens,
        reduced[0],
        reduced[1],
        reduced[2],
        reduced[3],
        reduced[4],
        reduced[5],
        reduced[6],
        reduced[7],
        reduced[8],
    )


def solution(mesh):
    in_specs = (
        P("fsdp", "ctx", None),
        P("fsdp", "ctx"),
        P(None, "fsdp"),
        P(None, "fsdp"),
        P(None, "fsdp", "tp"),
        P(None, "tp", "fsdp"),
        P("tp", "fsdp"),
        P(None, "fsdp"),
        P("fsdp", "tp"),
        P("tp", "fsdp"),
        P("tp", "fsdp"),
        P("fsdp", "ctx", None),
    )
    out_specs = (
        P("fsdp", "ctx", None),
        P("fsdp", "ctx", None),
        P(None, "fsdp"),
        P(None, "fsdp"),
        P(None, "fsdp", "tp"),
        P(None, "tp", "fsdp"),
        P("tp", "fsdp"),
        P(None, "fsdp"),
        P("fsdp", "tp"),
        P("tp", "fsdp"),
        P("tp", "fsdp"),
    )
    return jax.shard_map(local, mesh=mesh, in_specs=in_specs, out_specs=out_specs, check_vma=False)
```

profile of v0, /device:TPU:0, one launch (start us, length us, event | category | flops | bytes accessed | tf_op | source)
XLA Modules:
  0.0 1357.9 jit_solution(1582386412131539376)
XLA Ops:
  8.1 6.4 all-gather
  15.2 5.5 all-gather.1
  26.1 13.1 all_gather.39
  44.4 5.2 all_gather.40
  58.3 7.1 all_gather.43
  65.6 16.0 %all-gather.7.cloned.1.call-done = bf16[2,1024,384]{1,0,2:T(2,128)(2,1)} async-done(((bf16[2,512,384]{1,0,2:T(2,128)(2,1)}), bf16[2,1024,384]{1,0,2:T(2,128)(2,1)}) %all-gather.7.cloned.1.call-update) | async-done | bytes 1572880 | tf_op jit(solution)/shard_map/all_gather | solution.py:93
  84.5 11.8 while.28
  106.4 5.4 all_gather.46
  112.5 107.9 %all-reduce.8.cloned.1.call-done = f32[1024,768]{1,0:T(8,128)} async-done(((f32[1024,768]{1,0:T(8,128)}), f32[1024,768]{1,0:T(8,128)}) %all-reduce.8.cloned.1.call-update) | async-done | bytes 3145744 | tf_op jit(solution)/shard_map/psum | solution.py:35
  231.9 6.4 fusion.155
  242.9 119.9 %all-reduce.10.cloned.1.call-done = f32[1024,768]{1,0:T(8,128)} async-done(((f32[1024,768]{1,0:T(8,128)}), f32[1024,768]{1,0:T(8,128)}) %all-reduce.10.cloned.1.call-update) | async-done | bytes 3145744 | tf_op jit(solution)/shard_map/psum | solution.py:35
  372.2 73.1 %while.29 = (s32[]{:T(128)}, bf16[2,1024,3,64]{1,3,2,0:T(8,128)(2,1)}, bf16[2,1024,3,64]{1,3,2,0:T(8,128)(2,1)}, bf16[2,1,512,3,64]{2,4,3,1,0:T(8,128)(2,1)}, bf...) while((s32[]{:T(128)}, ...), condition=%wide.region_15.16_spmd.clone, body=%wide.region_13.15_spmd.clone.sunk | while | flops 1049105920 | bytes 106249448 | solution.py:218
  381.0 13.4 fusion.220
  394.4 14.2 %fusion.218 = bf16[2,1024,3,64]{1,3,2,0:T(8,128)(2,1)} fusion(bf16[2,1024,3,64]{1,3,2,0:T(8,128)(2,1)} %get-tuple-element.637, s32[]{:T(128)S(6)} %copy.159, f32[3,512,1024]{2,1,0:T(8,128)} %fusion.215, f32[3,512,1024]{2,1,0:T(8,128)} %copy-done, f32[3,512]{1,0:T(4,128)S(1)} %dynamic-slice_bitcast_fusion.2, pred[512,1024]{1,0:T(8,128)(4,1)S(1)} %fusion.217, ...), kind=kOutput, calls=%fused_computation.50.clone.1 | convolution fusion | flops 218630656 | bytes 27214848 | tf_op jit(solution)/shard_map/while/body/eval_jaxpr/while/body/eval_jaxpr/hqk,qhd->khd/dot_general | solution.py:199
  417.4 13.4 fusion.220
  430.8 14.2 %fusion.218 = bf16[2,1024,3,64]{1,3,2,0:T(8,128)(2,1)} fusion(bf16[2,1024,3,64]{1,3,2,0:T(8,128)(2,1)} %get-tuple-element.637, s32[]{:T(128)S(6)} %copy.159, f32[3,512,1024]{2,1,0:T(8,128)} %fusion.215, f32[3,512,1024]{2,1,0:T(8,128)} %copy-done, f32[3,512]{1,0:T(4,128)S(1)} %dynamic-slice_bitcast_fusion.2, pred[512,1024]{1,0:T(8,128)(4,1)S(1)} %fusion.217, ...), kind=kOutput, calls=%fused_computation.50.clone.1 | convolution fusion | flops 218630656 | bytes 27214848 | tf_op jit(solution)/shard_map/while/body/eval_jaxpr/while/body/eval_jaxpr/hqk,qhd->khd/dot_general | solution.py:199
  452.5 71.2 %copy.113 = bf16[2,1024,384]{0,2,1:T(8,128)(2,1)} copy(bf16[2,1024,384]{1,0,2:T(2,128)(2,1)} %pad_maximum_fusion) | data formatting | bytes 3145728
  523.6 162.7 %reshape.405 = bf16[1024,768]{1,0:T(8,128)(2,1)} reshape(bf16[1024,384,2]{2,1,0:T(8,128)(2,1)} %bitcast.53) | data formatting | bytes 3145728
  688.6 23.1 %reduce-scatter.31.cloned.1.call-done = bf16[512,768]{1,0:T(8,128)(2,1)} async-done(((bf16[1024,768]{1,0:T(8,128)(2,1)}), bf16[512,768]{1,0:T(8,128)(2,1)}) %reduce-scatter.31.cloned.1.call-update) | async-done | bytes 786448
  711.6 110.2 %reshape.406 = bf16[512,384,2]{2,1,0:T(8,128)(2,1)} reshape(bf16[512,768]{1,0:T(8,128)(2,1)} %reduce-scatter.31.cloned.1.call-done) | data formatting | bytes 1572864
  821.8 45.7 %copy.114 = bf16[2,512,384]{1,0,2:T(2,128)(2,1)S(1)} copy(bf16[2,512,384]{0,2,1:T(8,128)(2,1)} %bitcast.252) | data formatting | bytes 1572864
  890.0 10.7 reduce-scatter.37.cloned.1.call-done
  902.9 26.1 %reduce-scatter.29.cloned.1.call-done = bf16[768,192]{0,1:T(8,128)(2,1)} async-done(((bf16[768,768]{0,1:T(8,128)(2,1)}), bf16[768,192]{0,1:T(8,128)(2,1)}) %reduce-scatter.29.cloned.1.call-update) | async-done | bytes 294928 | tf_op jit(solution)/shard_map/reduce_scatter | solution.py:299
  928.9 28.8 %reduce-scatter.27.cloned.1.call-done = bf16[192,768]{1,0:T(8,128)(2,1)} async-done(((bf16[768,768]{1,0:T(8,128)(2,1)}), bf16[192,768]{1,0:T(8,128)(2,1)}) %reduce-scatter.27.cloned.1.call-update) | async-done | bytes 294928 | tf_op jit(solution)/shard_map/reduce_scatter | solution.py:293
  958.0 6.2 fusion.144
  967.4 12.2 reduce-scatter.45.cloned.1.call-done
  980.5 21.9 %reduce-scatter.43.cloned.1.call-done = bf16[192,2]{1,0:T(8,128)(2,1)} async-done(((bf16[768,2]{1,0:T(8,128)(2,1)}), bf16[192,2]{1,0:T(8,128)(2,1)}) %reduce-scatter.43.cloned.1.call-update) | async-done | bytes 784
  1003.2 21.1 %reduce-scatter.39.cloned.1.call-done = bf16[16,6]{1,0:T(8,128)(2,1)} async-done(((bf16[64,6]{1,0:T(8,128)(2,1)}), bf16[16,6]{1,0:T(8,128)(2,1)}) %reduce-scatter.39.cloned.1.call-update) | async-done | bytes 208
  1025.2 40.2 %all-reduce.14.cloned.1.call-done = (bf16[3,192,192]{1,2,0:T(8,128)(2,1)}, bf16[192,192]{1,0:T(8,128)(2,1)}, bf16[192,768]{1,0:T(8,128)(2,1)}, bf16[768,192]{0,1:T(8,128)(2,1)}) async-done(((bf16[3,192,192]{1,2,0:T(8,128)(2,1)}, bf16[192,192]{1,0:T(8,128)(2,1)}, bf16[192,768]{1,0:T(8,128)(2,1)}, bf16[768,192]{0,1:T(8,128)(2,1)}), (bf16[3,192,192]{1,2,0:T(8,128)(2,1)}, bf16[192,192]{1,0:T(8,128)(2,1)}, ...) | async-done | bytes 884752 | tf_op jit(solution)/shard_map/psum | solution.py:306
  1072.6 218.7 %all-reduce.12.cloned.1.call-done = (f32[1024,768]{1,0:T(8,128)}, f32[1024,768]{1,0:T(8,128)}) async-done(((f32[1024,768]{1,0:T(8,128)}, f32[1024,768]{1,0:T(8,128)}), (f32[1024,768]{1,0:T(8,128)}, f32[1024,768]{1,0:T(8,128)})) %all-reduce.12.cloned.1.call-update) | async-done | bytes 6291472 | tf_op jit(solution)/shard_map/psum | solution.py:35
  1304.8 14.4 %reduce-scatter.33.cloned.1.call-done = bf16[192,2]{1,0:T(8,128)(2,1)} async-done(((bf16[768,2]{1,0:T(8,128)(2,1)}), bf16[192,2]{1,0:T(8,128)(2,1)}) %reduce-scatter.33.cloned.1.call-update) | async-done | bytes 784
  1320.1 21.4 %reduce-scatter.35.cloned.1.call-done = bf16[192,2]{1,0:T(8,128)(2,1)} async-done(((bf16[768,2]{1,0:T(8,128)(2,1)}), bf16[192,2]{1,0:T(8,128)(2,1)}) %reduce-scatter.35.cloned.1.call-update) | async-done | bytes 784
  (335 shorter events, 158.0 us)
Async XLA Ops:
  8.0 17.9 %copy-start.34 = (bf16[3,192,192]{2,1,0:T(8,128)(2,1)S(1)}, bf16[3,192,192]{2,1,0:T(8,128)(2,1)}, u32[]{:S(2)}) copy-start(bf16[3,192,192]{2,1,0:T(8,128)(2,1)} %param.20) | copy-start | bytes 663556
  8.0 73.6 %all-gather.7.cloned.1.call-start = ((), (), s32[]{:S(2)}) async-start(), calls=%async_computation.10 | async-start | bytes 2359296 | tf_op jit(solution)/shard_map/all_gather | solution.py:93
  15.2 26.1 %copy-start.35 = (f32[768]{0:T(1024)}, f32[768]{0:T(1024)S(1)}, u32[]{:S(2)}) copy-start(f32[768]{0:T(1024)S(1)} %get-tuple-element.382) | copy-start | bytes 9220
  23.1 18.2 %copy-start.37 = (f32[1,4,2,128]{3,1,2,0:T(4,128)}, f32[1,4,2,128]{3,1,2,0:T(4,128)S(1)}, u32[]{:S(2)}) copy-start(f32[1,4,2,128]{3,1,2,0:T(4,128)S(1)} %copy.129) | copy-start | bytes 12292
  23.1 18.2 %copy-start.3 = (bf16[2,512,768]{2,1,0:T(8,128)(2,1)S(1)}, bf16[2,512,768]{2,1,0:T(8,128)(2,1)}, u32[]{:S(2)}) copy-start(bf16[2,512,768]{2,1,0:T(8,128)(2,1)} %param.16) | copy-start | bytes 4718596
  25.9 16.1 %copy-start.41 = (f32[1024]{0:T(1024)}, f32[1024]{0:T(1024)S(1)}, u32[]{:S(2)}) copy-start(f32[1024]{0:T(1024)S(1)} %rsqrt.21) | copy-start | bytes 12292
  44.3 13.3 copy-start.40
  53.0 167.5 %all-reduce.8.cloned.1.call-start = ((), (), s32[]{:S(2)}) async-start(), calls=%async_computation.11 | async-start | bytes 6291456 | tf_op jit(solution)/shard_map/psum | solution.py:35
  65.4 31.5 %copy-start.19 = (bf16[192,768]{0,1:T(8,128)(2,1)}, bf16[192,768]{0,1:T(8,128)(2,1)S(1)}, u32[]{:S(2)}) copy-start(bf16[192,768]{0,1:T(8,128)(2,1)S(1)} %all_gather.43) | copy-start | bytes 884740
  99.3 127.8 %all-gather.9.cloned.1.call-start = ((), (), s32[]{:S(2)}) async-start(), calls=%async_computation.12 | async-start | bytes 1474560 | tf_op jit(solution)/shard_map/all_gather | solution.py:59
  99.9 132.0 %all-gather.11.cloned.1.call-start = ((), (), s32[]{:S(2)}) async-start(), calls=%async_computation.13 | async-start | bytes 1474560 | tf_op jit(solution)/shard_map/all_gather | solution.py:61
  100.5 262.4 %all-reduce.10.cloned.1.call-start = ((), (), s32[]{:S(2)}) async-start(), calls=%async_computation.14 | async-start | bytes 6291456 | tf_op jit(solution)/shard_map/psum | solution.py:35
  223.3 143.2 %copy-start.1 = (f32[1024,768]{1,0:T(8,128)}, f32[1024,768]{1,0:T(8,128)S(1)}, u32[]{:S(2)}) copy-start(f32[1024,768]{1,0:T(8,128)S(1)} %get-tuple-element.443) | copy-start | bytes 9437188
  242.6 469.0 %reduce-scatter.31.cloned.1.call-start = ((), (), s32[]{:S(2)}) async-start(), calls=%async_computation.17 | async-start | bytes 2359296
  523.6 162.8 %copy-start.22 = (bf16[24,8,2,512]{3,1,2,0:T(8,128)(2,1)S(1)}, bf16[24,8,2,512]{3,1,2,0:T(8,128)(2,1)}, u32[]{:S(2)}) copy-start(bf16[24,8,2,512]{3,1,2,0:T(8,128)(2,1)} %copy-done.21) | copy-start | bytes 1179652
  686.3 202.1 %reduce-scatter.41.cloned.1.call-start = ((), (), s32[]{:S(2)}) async-start(), calls=%async_computation.22 | async-start | bytes 491520
  687.8 212.9 %reduce-scatter.37.cloned.1.call-start = ((), (), s32[]{:S(2)}) async-start(), calls=%async_computation.20 | async-start | bytes 1228800
  688.6 179.2 %copy-start.28 = (bf16[1,1024,192]{1,2,0:T(8,128)(2,1)}, bf16[1,1024,192]{1,2,0:T(8,128)(2,1)S(1)}, u32[]{:S(2)}) copy-start(bf16[1,1024,192]{1,2,0:T(8,128)(2,1)S(1)} %convert_element_type.214) | copy-start | bytes 1179652
  876.1 52.8 %reduce-scatter.29.cloned.1.call-start = ((), (), s32[]{:S(2)}) async-start(), calls=%async_computation.16 | async-start | bytes 1474560 | tf_op jit(solution)/shard_map/reduce_scatter | solution.py:299
  881.1 76.6 %reduce-scatter.27.cloned.1.call-start = ((), (), s32[]{:S(2)}) async-start(), calls=%async_computation.15 | async-start | bytes 1474560 | tf_op jit(solution)/shard_map/reduce_scatter | solution.py:293
  885.1 94.6 %reduce-scatter.45.cloned.1.call-start = ((), (), s32[]{:S(2)}) async-start(), calls=%async_computation.24 | async-start | bytes 20480
  886.2 116.1 %reduce-scatter.43.cloned.1.call-start = ((), (), s32[]{:S(2)}) async-start(), calls=%async_computation.23 | async-start | bytes 245760
  887.3 137.0 %reduce-scatter.39.cloned.1.call-start = ((), (), s32[]{:S(2)}) async-start(), calls=%async_computation.21 | async-start | bytes 20480
  888.3 177.0 %all-reduce.14.cloned.1.call-start = ((), (), s32[]{:S(2)}) async-start(), calls=%async_computation.26 | async-start | bytes 1966080 | tf_op jit(solution)/shard_map/psum | solution.py:306
  957.8 333.5 %all-reduce.12.cloned.1.call-start = ((), (), s32[]{:S(2)}) async-start(), calls=%async_computation.25 | async-start | bytes 12582912 | tf_op jit(solution)/shard_map/psum | solution.py:35
  967.3 324.0 %copy-start.4 = (bf16[2,512,768]{2,1,0:T(8,128)(2,1)S(1)}, bf16[2,512,768]{2,1,0:T(8,128)(2,1)}, u32[]{:S(2)}) copy-start(bf16[2,512,768]{2,1,0:T(8,128)(2,1)} %param.16) | copy-start | bytes 4718596
  967.3 324.0 %copy-start.36 = (f32[768]{0:T(1024)S(1)}, f32[768]{0:T(1024)}, u32[]{:S(2)}) copy-start(f32[768]{0:T(1024)} %copy-done.35) | copy-start | bytes 9220
  967.3 324.0 %copy-start.38 = (f32[1,4,2,128]{3,1,2,0:T(4,128)S(1)}, f32[1,4,2,128]{3,1,2,0:T(4,128)}, u32[]{:S(2)}) copy-start(f32[1,4,2,128]{3,1,2,0:T(4,128)} %copy-done.37) | copy-start | bytes 12292
  967.4 351.9 %reduce-scatter.33.cloned.1.call-start = ((), (), s32[]{:S(2)}) async-start(), calls=%async_computation.18 | async-start | bytes 245760
  1068.9 225.4 %copy-start.52 = (f32[1,4,2,128]{3,1,2,0:T(4,128)S(1)}, f32[1,4,2,128]{3,1,2,0:T(4,128)}, u32[]{:S(2)}) copy-start(f32[1,4,2,128]{3,1,2,0:T(4,128)} %copy-done.51) | copy-start | bytes 12292
  1068.9 225.4 %copy-start.42 = (f32[1024]{0:T(1024)S(1)}, f32[1024]{0:T(1024)}, u32[]{:S(2)}) copy-start(f32[1024]{0:T(1024)} %copy-done.41) | copy-start | bytes 12292
  1300.4 41.1 %reduce-scatter.35.cloned.1.call-start = ((), (), s32[]{:S(2)}) async-start(), calls=%async_computation.19 | async-start | bytes 245760
  (54 other events, 193.7 us)
Sparse Core Ops, SparseCore 0:
  53.1 28.4 all-gather.6
  99.4 121.0 all-reduce.7
  242.7 120.0 all-reduce.9
  686.4 25.1 reduce-scatter.30
  714.0 20.8 reduce-scatter.40
  876.3 24.4 reduce-scatter.36
  903.3 25.5 reduce-scatter.28
  932.1 25.6 reduce-scatter.26
  960.1 19.5 reduce-scatter.44
  982.5 19.7 reduce-scatter.42
  1004.8 19.4 reduce-scatter.38
  1026.7 38.6 all-reduce.13
  1068.4 222.8 all-reduce.11
Sparse Core Ops, SparseCore 1:
  101.3 17.3 all-gather.8
  120.1 17.2 all-gather.10
  1300.5 18.7 reduce-scatter.32
  1321.7 19.8 reduce-scatter.34
where the time goes:
time: 1370 us; the launch traced here: 1360 us
  waiting for transfers between devices  684 us (50%)
  local copies, waits for them, and re-layouts  436 us (32%)
  matrix products  116 us (8%)
  blocking collectives  57.1 us (4%)
  other arithmetic  46.8 us (3%)
  between operations  16.9 us (1%)
    psum x3, waiting for transfers between devices, tp_total(): return lax.psum(make(0, row_count), 'tp')  447 us
    unnamed x159, local copies, waits for them, and re-layouts  418 us
    unnamed x25, waiting for transfers between devices  126 us
    psum x1, waiting for transfers between devices, local(): lax.psum(part_qkv.astype(jnp.bfloat16), 'ctx').astype(jnp.float32)  40.2 us
    reduce_scatter x1, waiting for transfers between devices, local(): lax.psum_scatter(grad_up.astype(jnp.bfloat16), 'fsdp', scatter_dimension=...  28.8 us
    dot_general x2, matrix products, backward_block(): jnp.einsum('hqk,qhd->khd', grad_scores, queries, preferred_element_type=j...  28.4 us
  transfers between devices with their start and end apart: 17, of which 14 were waited for; matrix products, arithmetic and copies ran while one was open for 16% of the time, Pallas kernels for 0%

commit v1 on v0

v1 whole, which is shorter than its diff:
```python
import functools
import math

import jax
import jax.numpy as jnp
from jax import lax
from jax.experimental import pallas as pl
from jax.experimental.pallas import tpu as pltpu
from jax.sharding import PartitionSpec as P

HD = 64
QB = 256
eps = 1e-05
masked_score = -1e30
score_scale = 0.125 * math.log2(math.e)
f32 = jnp.float32
bf16 = jnp.bfloat16


def swap(v, axis, bit, size):
    return lax.ppermute(v, axis, [(i, i ^ bit) for i in range(size)])


def dot(a, b):
    return lax.dot_general(a, b, (((1,), (0,)), ((), ())), preferred_element_type=f32)


def turned(v):
    return v.astype(f32).T.astype(v.dtype)


def starts_of(seg):
    start = jnp.zeros(seg.shape, jnp.int32)
    for number in range(3):
        count = jnp.sum((seg == number).astype(jnp.int32), axis=1, keepdims=True)
        start = start + jnp.where(seg > number, count, 0)
    return start


def allowed_block(start, first, width):
    place = lax.broadcasted_iota(jnp.int32, (width, QB), 0)
    allowed = place >= start[:, first : first + QB]
    query = lax.broadcasted_iota(jnp.int32, (width, QB), 1) + first
    return allowed & (place <= query)


def attention_forward(seg_ref, qkv_ref, out_ref, log_ref):
    start = starts_of(seg_ref[...])
    length = qkv_ref.shape[2]
    heads = qkv_ref.shape[1] // HD
    for head in range(heads):
        rows = slice(head * HD, (head + 1) * HD)
        keys = turned(qkv_ref[1, rows, :])
        for first in range(0, length, QB):
            width = first + QB
            cols = slice(first, first + QB)
            scores = dot(keys[:width], qkv_ref[0, rows, cols]) * score_scale
            scores = jnp.where(allowed_block(start, first, width), scores, masked_score)
            top = jnp.max(scores, axis=0, keepdims=True)
            weight = jnp.exp2(scores - top)
            total = jnp.sum(weight, axis=0, keepdims=True)
            mixed = dot(qkv_ref[2, rows, :width], weight.astype(bf16))
            out_ref[rows, cols] = (mixed / total).astype(bf16)
            log_ref[head : head + 1, cols] = top + jnp.log2(total)


def attention_backward(seg_ref, qkv_ref, grad_ref, log_ref, out_ref, key_sum, value_sum):
    start = starts_of(seg_ref[...])
    length = qkv_ref.shape[2]
    width_heads = qkv_ref.shape[1]
    for head in range(width_heads // HD):
        rows = slice(head * HD, (head + 1) * HD)
        keys = turned(qkv_ref[1, rows, :])
        values = turned(qkv_ref[2, rows, :])
        queries = turned(qkv_ref[0, rows, :])
        grads = turned(grad_ref[rows, :])
        key_sum[...] = jnp.zeros_like(key_sum)
        value_sum[...] = jnp.zeros_like(value_sum)
        for first in range(0, length, QB):
            width = first + QB
            cols = slice(first, first + QB)
            scores = dot(keys[:width], qkv_ref[0, rows, cols]) * score_scale
            prob = jnp.exp2(scores - log_ref[head : head + 1, cols])
            prob = jnp.where(allowed_block(start, first, width), prob, 0.0)
            grad_prob = dot(values[:width], grad_ref[rows, cols])
            inner = jnp.sum(prob * grad_prob, axis=0, keepdims=True)
            grad_scores = (prob * (grad_prob - inner) * 0.125).astype(bf16)
            grad_query = dot(qkv_ref[1, rows, :width], grad_scores)
            out_ref[cols, rows] = grad_query.T.astype(bf16)
            key_sum[:width] += dot(grad_scores, queries[cols])
            value_sum[:width] += dot(prob.astype(bf16), grads[cols])
        out_ref[:, width_heads + head * HD : width_heads + (head + 1) * HD] = key_sum[...].astype(bf16)
        out_ref[:, 2 * width_heads + head * HD : 2 * width_heads + (head + 1) * HD] = value_sum[
            ...
        ].astype(bf16)


def normalized(v):
    mean = jnp.mean(v, axis=-1, keepdims=True)
    centered = v - mean
    scale = lax.rsqrt(jnp.mean(centered * centered, axis=-1, keepdims=True) + eps)
    return centered * scale, scale


def norm_back(hat, scale, gain, grad):
    scaled = grad * gain
    first = jnp.mean(scaled, axis=-1, keepdims=True)
    second = jnp.mean(scaled * hat, axis=-1, keepdims=True)
    return scale * (scaled - first - hat * second)


def gelu_pair(u):
    slope = math.sqrt(2 / math.pi)
    bent = jnp.tanh(slope * (u + 0.044715 * u * u * u))
    value = 0.5 * u * (1 + bent)
    rate = 0.5 * (1 + bent) + 0.5 * u * (1 - bent * bent) * slope * (1 + 3 * 0.044715 * u * u)
    return value, rate


def arranged(parts, at):
    low, high = (at & 1) == 1, (at >> 1) == 1
    p0, p1, p2, p3 = parts
    a0, a1 = jnp.where(low, p1, p0), jnp.where(low, p0, p1)
    a2, a3 = jnp.where(low, p3, p2), jnp.where(low, p2, p3)
    return [
        jnp.where(high, a2, a0),
        jnp.where(high, a3, a1),
        jnp.where(high, a0, a2),
        jnp.where(high, a1, a3),
    ]


def pick(v, index, axis):
    return lax.dynamic_index_in_dim(v, index, axis, keepdims=False)


def block(
    tokens,
    segments,
    ln_gains,
    ln_biases,
    w_qkv,
    bias_qv,
    w_out,
    out_biases,
    w_up,
    up_bias,
    w_down,
    cotangent,
    *,
    fsdp,
    ctx,
    tp,
):
    seq_count, half, width = tokens.shape
    part = w_up.shape[0]
    heads_width = w_qkv.shape[2]
    head_count = heads_width // HD
    hidden_part = w_up.shape[1]
    assert ctx == 2 and seq_count == 2 and tp == 4
    f = lax.axis_index("fsdp")
    y = lax.axis_index("ctx")
    z = lax.axis_index("tp")
    piece = half // tp
    pair = z >> 1
    member = z & 1

    def swap_y(v):
        return swap(v, "ctx", 1, ctx)

    def swap_z(v, bit):
        return swap(v, "tp", bit, tp)

    def gather_rows(v):
        if fsdp != 4:
            return lax.all_gather(v, "fsdp", axis=0, tiled=True).reshape((fsdp,) + v.shape)
        far = swap(v, "fsdp", 2, fsdp)
        near = swap(v, "fsdp", 1, fsdp)
        cross = swap(far, "fsdp", 1, fsdp)
        return arranged([v, near, far, cross], f)

    def scatter_rows(g):
        g = g.astype(bf16)
        if fsdp != 4:
            return lax.psum_scatter(g, "fsdp", scatter_dimension=0, tiled=True).astype(f32)
        g = g.reshape(2, 2, part, g.shape[1])
        core, x = f & 1, f >> 1
        kept = pick(g, core, 1)
        got = swap(pick(g, 1 - core, 1), "fsdp", 1, fsdp)
        send = (pick(kept, 1 - x, 0).astype(f32) + pick(got, 1 - x, 0).astype(f32)).astype(bf16)
        own = pick(kept, x, 0).astype(f32) + pick(got, x, 0).astype(f32)
        return own + swap(send, "fsdp", 2, fsdp).astype(f32)

    def sum_y(g):
        g = g.astype(bf16)
        return g.astype(f32) + swap_y(g).astype(f32)

    tok_own = pick(tokens, y, 0)
    tok_got = swap_y(pick(tokens, 1 - y, 0))
    small = jnp.concatenate(
        [
            ln_gains.reshape(-1),
            ln_biases.reshape(-1),
            out_biases.reshape(-1),
            up_bias.reshape(-1),
            bias_qv.reshape(-1),
        ]
    )
    small_rows = -(-small.shape[0] // heads_width)
    small = jnp.pad(small, (0, small_rows * heads_width - small.shape[0]))
    qkv_pack = jnp.concatenate(
        [w_qkv.reshape(3 * part, heads_width), small.reshape(small_rows, heads_width)], axis=0
    )
    packs = gather_rows(qkv_pack)
    cot_rows = lax.dynamic_slice_in_dim(cotangent, pair * 2 * piece, 2 * piece, 1)
    seg_row = jnp.pad(pick(segments, 1 - y, 0).astype(bf16), (0, width - half)).reshape(1, width)
    extra_got = swap_y(jnp.concatenate([pick(cot_rows, 1 - y, 0), seg_row], axis=0))
    up_bias_far = swap_z(up_bias, 2)
    mlp_pack = jnp.concatenate([w_up, w_down.T], axis=0)
    mlp_far = swap_z(mlp_pack, 2)
    out_turned = w_out.T
    out_two = jnp.concatenate([out_turned, swap_z(out_turned, 1)], axis=1)
    out_four = jnp.concatenate([out_two, swap_z(out_two, 2)], axis=1)

    packs = [packs[i] for i in range(fsdp)]
    qkv_proj = jnp.concatenate(
        [p[: 3 * part].reshape(3, part, heads_width) for p in packs], axis=1
    )
    flat = jnp.stack([p[3 * part :].reshape(-1) for p in packs]).astype(f32)
    norms = jnp.moveaxis(flat[:, : 6 * part].reshape(fsdp, 6, part), 0, 1).reshape(6, width)
    gains, shifts, branch_bias = norms[0:2], norms[2:4], norms[4:6]
    base = 6 * part
    bias_rows, bias_cols = up_bias.shape
    up_shift = jnp.moveaxis(
        flat[:, base : base + bias_rows * bias_cols].reshape(fsdp, bias_rows, bias_cols), 0, 1
    ).reshape(-1)
    base = base + bias_rows * bias_cols
    qv_cols = bias_qv.shape[2]
    qv_bias = jnp.moveaxis(
        flat[:, base : base + 2 * head_count * qv_cols].reshape(fsdp, 2, head_count, qv_cols), 0, 2
    ).reshape(2, heads_width)
    up_far = gather_rows(jnp.pad(up_bias_far.reshape(1, -1), ((0, 0), (0, 0))))
    up_shift_far = jnp.moveaxis(
        jnp.stack([up_far[i].reshape(bias_rows, bias_cols) for i in range(fsdp)]), 0, 1
    ).reshape(-1).astype(f32)

    first_half = jnp.where(y == 0, tok_own, tok_got)
    second_half = jnp.where(y == 0, tok_got, tok_own)
    inputs = jnp.concatenate([first_half, second_half], axis=0).astype(f32)
    length = inputs.shape[0]
    seg_own = pick(segments, y, 0).astype(f32)
    seg_got = extra_got[2 * piece, :half].astype(f32)
    seg = jnp.concatenate(
        [jnp.where(y == 0, seg_own, seg_got), jnp.where(y == 0, seg_got, seg_own)]
    ).reshape(1, length).astype(jnp.int32)
    hat, _ = normalized(inputs)
    normed = (hat * gains[0] + shifts[0]).astype(bf16)
    projected = jnp.einsum("cdh,td->cht", qkv_proj, normed, preferred_element_type=f32)
    shift_rows = jnp.stack([qv_bias[0], jnp.zeros_like(qv_bias[0]), qv_bias[1]])
    qkv = (projected + shift_rows[:, :, None]).astype(bf16)
    attended, logs = pl.pallas_call(
        attention_forward,
        out_shape=(
            jax.ShapeDtypeStruct((heads_width, length), bf16),
            jax.ShapeDtypeStruct((head_count, length), f32),
        ),
        name="attention_forward",
    )(seg, qkv)

    def pieces_of(v):
        v = v.reshape(heads_width, 2, tp, piece)
        return [pick(v, z ^ k, 2).reshape(heads_width, 2 * piece) for k in range(tp)]

    att_pieces = pieces_of(attended)
    att_all = jnp.concatenate(
        [att_pieces[0]] + [swap_z(att_pieces[k], k) for k in range(1, tp)], axis=0
    )
    out_proj = jnp.concatenate([v for v in gather_rows(out_four)], axis=0)
    rows_own = lax.dynamic_slice_in_dim(inputs.reshape(2, half, width), z * piece, piece, 1).reshape(
        2 * piece, width
    )
    branch = jnp.einsum("ht,dh->td", att_all, out_proj, preferred_element_type=f32)
    hidden = rows_own + branch + branch_bias[0]
    hat_two, scale_two = normalized(hidden)
    normed_own = (hat_two * gains[1] + shifts[1]).astype(bf16)
    normed_two = jnp.concatenate([normed_own, swap_z(normed_own, 1)], axis=0)

    mlp = []
    for pack, shift in ((mlp_pack, up_shift), (mlp_far, up_shift_far)):
        got = gather_rows(pack)
        up = jnp.concatenate([got[i][:part] for i in range(fsdp)], axis=0)
        down = jnp.concatenate([got[i][part:] for i in range(fsdp)], axis=0)
        mlp.append((up, down, shift))
    cot_own = pick(cot_rows, y, 0)
    cot_got = extra_got[: 2 * piece]
    cot_two = jnp.stack(
        [jnp.where(y == 0, cot_own, cot_got), jnp.where(y == 0, cot_got, cot_own)]
    ).reshape(2, 2, piece, width)
    cot_near = pick(cot_two, member, 1).reshape(2 * piece, width)
    cot_far = pick(cot_two, 1 - member, 1).reshape(2 * piece, width)
    cot_pair = jnp.concatenate([cot_near, cot_far], axis=0)
    acts, grads_pre = [], []
    for up, down, shift in mlp:
        pre = jnp.dot(normed_two, up, preferred_element_type=f32) + shift
        value, rate = gelu_pair(pre)
        acts.append(value.astype(bf16))
        grad_act = jnp.dot(cot_pair, down, preferred_element_type=f32).astype(bf16)
        grads_pre.append((grad_act.astype(f32) * rate).astype(bf16))
    back = sum(
        jnp.einsum("tf,df->td", g, m[0], preferred_element_type=f32)
        for g, m in zip(grads_pre, mlp)
    )
    own_rows = 2 * piece
    grad_normed_two = back[:own_rows] + swap_z(back[own_rows:].astype(bf16), 1).astype(f32)
    cot_own_rows = cot_near.astype(f32)
    grad_hidden = cot_own_rows + norm_back(hat_two, scale_two, gains[1], grad_normed_two)
    grad_branch = grad_hidden.astype(bf16)
    grad_att = jnp.einsum("dh,td->ht", out_proj, grad_branch, preferred_element_type=f32).astype(
        bf16
    )
    grad_att = grad_att.reshape(tp, heads_width, 2, piece)
    grad_parts = [grad_att[0]] + [swap_z(grad_att[k], k) for k in range(1, tp)]
    grad_full = jnp.stack(arranged(grad_parts, z), axis=2).reshape(heads_width, length)

    down_sum = sum(
        jnp.einsum("tf,df->td", a, m[1], preferred_element_type=f32) for a, m in zip(acts, mlp)
    )
    second = down_sum[:own_rows] + swap_z(down_sum[own_rows:].astype(bf16), 1).astype(f32)
    result_rows = (hidden + second + branch_bias[1]).astype(bf16)

    def spread(rows):
        rows = rows.reshape(2, piece, width)
        mine = pick(rows, y, 0)
        other = swap_y(pick(rows, 1 - y, 0))
        both = jnp.stack([jnp.where(y == 0, mine, other), jnp.where(y == 0, other, mine)])
        far = swap_z(both, 2)
        near = swap_z(both, 1)
        cross = swap_z(far, 1)
        return jnp.concatenate(arranged([both, near, far, cross], z), axis=1)

    result = spread(result_rows)

    mlp_grads = []
    for a, g in zip(acts, grads_pre):
        grad_up = jnp.einsum("td,tf->df", normed_two, g, preferred_element_type=f32)
        grad_down = jnp.einsum("td,tf->df", cot_pair, a, preferred_element_type=f32)
        mlp_grads.append((scatter_rows(grad_up), scatter_rows(grad_down)))
    grad_up = sum_y(mlp_grads[0][0] + swap_z(mlp_grads[1][0].astype(bf16), 2).astype(f32))
    grad_down = sum_y(mlp_grads[0][1] + swap_z(mlp_grads[1][1].astype(bf16), 2).astype(f32)).T
    up_sums = [jnp.sum(g.astype(f32), axis=0) for g in grads_pre]
    up_bias_sum = up_sums[0] + swap_z(up_sums[1].reshape(1, -1), 2).reshape(-1)
    grad_out = scatter_rows(
        jnp.einsum("td,ht->dh", grad_branch, att_all, preferred_element_type=f32)
    )
    two = 2 * heads_width
    grad_out = grad_out[:, :two] + swap_z(grad_out[:, two:].astype(bf16), 2).astype(f32)
    grad_out = grad_out[:, :heads_width] + swap_z(
        grad_out[:, heads_width:].astype(bf16), 1
    ).astype(f32)
    grad_out = sum_y(grad_out).T

    grad_qkv_rows = pl.pallas_call(
        attention_backward,
        out_shape=jax.ShapeDtypeStruct((length, 3 * heads_width), bf16),
        scratch_shapes=[pltpu.VMEM((length, HD), f32), pltpu.VMEM((length, HD), f32)],
        name="attention_backward",
    )(seg, qkv, grad_full, logs)
    proj_rows = jnp.moveaxis(qkv_proj, 1, 0).reshape(width, 3 * heads_width)
    normed_grad = jnp.einsum("tc,dc->td", grad_qkv_rows, proj_rows, preferred_element_type=f32)
    normed_grad = normed_grad.reshape(2, tp, piece, width)
    grad_normed = pick(normed_grad, z, 1)
    for k in range(1, tp):
        grad_normed = grad_normed + swap_z(pick(normed_grad, z ^ k, 1).astype(bf16), k).astype(f32)
    grad_normed = grad_normed.reshape(own_rows, width)
    hat_one, scale_one = normalized(rows_own)
    token_rows = grad_hidden + norm_back(hat_one, scale_one, gains[0], grad_normed)
    grad_tokens = spread(token_rows.astype(bf16)).astype(f32)
    grad_qkv = sum_y(
        scatter_rows(jnp.einsum("td,tc->dc", normed, grad_qkv_rows, preferred_element_type=f32))
    )
    grad_qkv = jnp.moveaxis(grad_qkv.reshape(part, 3, heads_width), 1, 0)

    qkv_sums = jnp.sum(grad_qkv_rows.astype(f32), axis=0)
    qv_sums = jnp.concatenate([qkv_sums[:heads_width], qkv_sums[2 * heads_width :]])
    sums = jnp.stack(
        [
            jnp.sum(grad_normed * hat_one, axis=0),
            jnp.sum(grad_normed_two * hat_two, axis=0),
            jnp.sum(grad_normed, axis=0),
            jnp.sum(grad_normed_two, axis=0),
            jnp.sum(grad_branch.astype(f32), axis=0),
            jnp.sum(cot_own_rows, axis=0),
        ]
    )
    sums = sums + swap_z(sums, 1)
    sums = sums + swap_z(sums, 2)
    sums = jnp.concatenate(
        [sums, up_bias_sum.reshape(1, -1), jnp.pad(qv_sums, (0, width - 2 * heads_width))[None]]
    )
    if fsdp == 4:
        sums = sums + swap(sums, "fsdp", 1, fsdp)
        sums = sums + swap(sums, "fsdp", 2, fsdp)
    else:
        sums = lax.psum(sums, "fsdp")
    sums = sums + swap_y(sums)
    norm_sums = pick(sums[:6].reshape(6, fsdp, part), f, 1)
    grad_up_bias = pick(sums[6].reshape(bias_rows, fsdp, bias_cols), f, 1)
    grad_qv = pick(sums[7, : 2 * heads_width].reshape(2, head_count, fsdp, qv_cols), f, 2)
    return (
        result,
        grad_tokens,
        norm_sums[0:2],
        norm_sums[2:4],
        grad_qkv,
        grad_qv,
        grad_out,
        norm_sums[4:6],
        grad_up,
        grad_up_bias,
        grad_down,
    )


def solution(mesh):
    in_specs = (
        P("fsdp", "ctx", None),
        P("fsdp", "ctx"),
        P(None, "fsdp"),
        P(None, "fsdp"),
        P(None, "fsdp", "tp"),
        P(None, "tp", "fsdp"),
        P("tp", "fsdp"),
        P(None, "fsdp"),
        P("fsdp", "tp"),
        P("tp", "fsdp"),
        P("tp", "fsdp"),
        P("fsdp", "ctx", None),
    )
    out_specs = (
        P("fsdp", "ctx", None),
        P("fsdp", "ctx", None),
        P(None, "fsdp"),
        P(None, "fsdp"),
        P(None, "fsdp", "tp"),
        P(None, "tp", "fsdp"),
        P("tp", "fsdp"),
        P(None, "fsdp"),
        P("fsdp", "tp"),
        P("tp", "fsdp"),
        P("tp", "fsdp"),
    )
    local = functools.partial(
        block, fsdp=mesh.shape["fsdp"], ctx=mesh.shape["ctx"], tp=mesh.shape["tp"]
    )
    return jax.shard_map(local, mesh=mesh, in_specs=in_specs, out_specs=out_specs, check_vma=False)
```

time: 1370 us -> 340 us (0.25)
  waiting for transfers between devices: 684 us -> 141 us
  local copies, waits for them, and re-layouts: 436 us -> 34.8 us
  matrix products: 116 us -> 24 us
  blocking collectives: 57.1 us -> 0 us
  starting transfers between devices: 1.13 us -> 57 us
  Pallas kernels: 0 us -> 18.7 us
  between operations: 16.9 us -> 2.4 us
    psum x4 -> x0, waiting for transfers between devices: 487 us -> none  [the longest x3 447 us: tp_total(): return lax.psum(make(0, row_count), 'tp')]
    unnamed x159 -> x106, local copies, waits for them, and re-layouts: 418 us -> 8.04 us
    ppermute x0 -> x67, waiting for transfers between devices: none -> 141 us  [swap(): return lax.ppermute(v, axis, [(i, i ^ bit) for i in range(size)])]
    unnamed x25 -> x0, waiting for transfers between devices: 126 us -> none
    dot_general x25 -> x18, matrix products: 115 us -> 24 us  [the longest x1 4.23 us: block(): jnp.einsum('cdh,td->cht', qkv_proj, normed, preferred_element_type=f32)]
    ppermute x0 -> x67, starting transfers between devices: none -> 57 us  [swap(): return lax.ppermute(v, axis, [(i, i ^ bit) for i in range(size)])]
    reduce_scatter x2 -> x0, waiting for transfers between devices: 54.9 us -> none  [the longest x1 28.8 us: local(): lax.psum_scatter(grad_up.astype(jnp.bfloat16), 'fsdp', scatter_dimension=...]
    all_gather x8 -> x0, blocking collectives: 52.1 us -> none  [the longest x1 13.1 us: local(): lax.all_gather(w_qkv, 'fsdp', axis=1, tiled=True)]
  transfers between devices with their start and end apart: 17 -> 67, of which waited for: 14 -> 28; matrix products, arithmetic and copies ran while one was open for 16% -> 31% of each run, Pallas kernels for 0% -> 6%
where the time goes in v1:
time: 340 us; the launch traced here: 334 us
  waiting for transfers between devices  141 us (41%)
  starting transfers between devices  57 us (17%)
  other arithmetic  56 us (16%)
  local copies, waits for them, and re-layouts  34.8 us (10%)
  matrix products  24 us (7%)
  Pallas kernels  18.7 us (6%)
    ppermute x67, waiting for transfers between devices, swap(): return lax.ppermute(v, axis, [(i, i ^ bit) for i in range(size)])  141 us
    ppermute x67, starting transfers between devices, swap(): return lax.ppermute(v, axis, [(i, i ^ bit) for i in range(size)])  57 us
    pallas_call x1, Pallas kernels, block(): pl.pallas_call(attention_backward, out_shape=jax.ShapeDtypeStruct((length...  11 us
    select_n x7, other arithmetic, arranged(): jnp.where(high, a2, a0)  8.72 us
    unnamed x106, local copies, waits for them, and re-layouts  8.04 us
    convert_element_type x6, other arithmetic, scatter_rows(): (pick(kept, 1 - x, 0).astype(f32) + pick(got, 1 - x, 0).astype(f32)).asty...  7.88 us
    pallas_call x1, Pallas kernels, block(): pl.pallas_call(attention_forward, out_shape=(jax.ShapeDtypeStruct((heads_...  7.66 us
  transfers between devices with their start and end apart: 67, of which 28 were waited for; matrix products, arithmetic and copies ran while one was open for 31% of the time, Pallas kernels for 6%

profile of v1, /device:TPU:0, one launch (start us, length us, event | category | flops | bytes accessed | tf_op | source)
XLA Modules:
  0.0 333.7 jit_solution(13781405273999876138)
XLA Ops:
  6.5 3.0 collective-permute-start.2
  9.5 2.6 collective-permute-start.21
  19.6 3.0 collective-permute-done.22
  25.7 10.3 %collective-permute-done.9 = bf16[192,384]{0,1:T(8,128)(2,1)S(1)} collective-permute-done((bf16[192,384]{0,1:T(8,128)(2,1)S(1)}, bf16[192,384]{0,1:T(8,128)(2,1)S(1)}, u32[]{:S(2)}, u32[]{:S(2)}) %collective-permute-start.9) | collective-permute-done | bytes 147488 | tf_op jit(solution)/shard_map/ppermute | solution.py:21
  50.1 3.1 collective-permute-done.10
  53.2 11.0 %collective-permute-done.17 = bf16[384,768]{1,0:T(8,128)(2,1)} collective-permute-done((bf16[384,768]{1,0:T(8,128)(2,1)}, bf16[384,768]{1,0:T(8,128)(2,1)}, u32[]{:S(2)}, u32[]{:S(2)}) %collective-permute-start.17) | collective-permute-done | bytes 589856 | tf_op jit(solution)/shard_map/ppermute | solution.py:21
  69.0 4.2 %add_convert_fusion.1.qkv_ref = bf16[3,192,1024]{2,1,0:T(8,128)(2,1)} fusion(bf16[3,768,192]{1,2,0:T(8,128)(2,1)S(1)} %pad_maximum_fusion.7, f32[3,192]{1,0:T(4,128)S(1)} %pad_maximum_fusion.29, f32[768]{0:T(1024)S(1)} %copy-done.39, f32[768]{0:T(1024)S(1)} %mul.220, f32[1024]{0:T(1024)S(1)} %add_rsqrt_fusion, f32[1024]{0:T(1024)S(1)} %broadcast_multiply_fusion, ...), kind=kOutput, calls=%fused_computation.8 | convolution fusion | flops 914227200 | bytes 3653888 | tf_op jit(solution)/shard_map/cdh,td->cht/dot_general | solution.py:258
  74.1 7.7 %attention_forward.1 = (bf16[192,1024]{1,0:T(8,128)(2,1)}, f32[3,1024]{1,0:T(4,128)}) custom-call(s32[1,1024]{1,0:T(1,128)} %maximum_convert_fusion.2.seg_ref, bf16[3,192,1024]{2,1,0:T(8,128)(2,1)} %add_convert_fusion.1.qkv_ref), custom_call_target="tpu_custom_call" | custom-call | tf_op jit(solution)/shard_map/attention_forward/pallas_call | solution.py:261
  84.3 2.7 dynamic-slice_reduce_fusion
  89.4 3.2 collective-permute-done.5
  94.1 5.5 %collective-permute-done.6 = bf16[192,256]{1,0:T(8,128)(2,1)S(1)} collective-permute-done((bf16[192,256]{1,0:T(8,128)(2,1)S(1)}, bf16[192,256]{1,0:T(8,128)(2,1)S(1)}, u32[]{:S(2)}, u32[]{:S(2)}) %collective-permute-start.6) | collective-permute-done | bytes 98336 | tf_op jit(solution)/shard_map/ppermute | solution.py:21
  99.6 2.7 collective-permute-start.7
  102.3 3.7 %collective-permute-done.7 = bf16[192,256]{1,0:T(8,128)(2,1)S(1)} collective-permute-done((bf16[192,256]{1,0:T(8,128)(2,1)S(1)}, bf16[192,256]{1,0:T(8,128)(2,1)S(1)}, u32[]{:S(2)}, u32[]{:S(2)}) %collective-permute-start.7) | collective-permute-done | bytes 98336 | tf_op jit(solution)/shard_map/ppermute | solution.py:21
  110.0 7.1 %collective-permute-done.13 = bf16[256,768]{1,0:T(8,128)(2,1)S(1)} collective-permute-done((bf16[256,768]{1,0:T(8,128)(2,1)S(1)}, bf16[256,768]{1,0:T(8,128)(2,1)S(1)}, u32[]{:S(2)}, u32[]{:S(2)}) %collective-permute-start.13) | collective-permute-done | bytes 393248 | tf_op jit(solution)/shard_map/ppermute | solution.py:21
  138.0 9.9 %collective-permute-done.43 = f32[1,768]{1,0:T(1,128)S(1)} collective-permute-done((f32[1,768]{1,0:T(1,128)S(1)}, f32[1,768]{1,0:T(1,128)S(1)}, u32[]{:S(2)}, u32[]{:S(2)}) %collective-permute-start.43) | collective-permute-done | bytes 3104 | tf_op jit(solution)/shard_map/ppermute | solution.py:21
  152.6 2.8 collective-permute-start.31
  155.4 2.5 collective-permute-start.32
  161.4 4.1 %collective-permute-done.32 = bf16[192,2,128]{2,0,1:T(8,128)(2,1)S(1)} collective-permute-done((bf16[192,2,128]{2,0,1:T(8,128)(2,1)S(1)}, bf16[192,2,128]{2,0,1:T(8,128)(2,1)S(1)}, u32[]{:S(2)}, u32[]{:S(2)}) %collective-permute-start.32) | collective-permute-done | bytes 98336 | tf_op jit(solution)/shard_map/ppermute | solution.py:21
  167.9 11.0 %attention_backward.1 = bf16[1024,576]{1,0:T(8,128)(2,1)} custom-call(s32[1,1024]{1,0:T(1,128)} %maximum_convert_fusion.2.seg_ref, bf16[3,192,1024]{2,1,0:T(8,128)(2,1)} %add_convert_fusion.1.qkv_ref, bf16[192,1024]{1,0:T(8,128)(2,1)} %reshape.437.grad_ref, f32[3,1024]{1,0:T(4,128)} %get-tuple-element.14.log_ref), custom_call_target="tpu_custom_call" | custom-call | tf_op jit(solution)/shard_map/attention_backward/pallas_call | solution.py:362
  180.5 3.0 fusion.96
  186.2 2.7 collective-permute-start.36
  189.0 2.7 convolution_convert_fusion.5
  201.9 19.6 %collective-permute-done.35 = bf16[2,128,768]{2,1,0:T(8,128)(2,1)S(1)} collective-permute-done((bf16[2,128,768]{2,1,0:T(8,128)(2,1)}, bf16[2,128,768]{2,1,0:T(8,128)(2,1)S(1)}, u32[]{:S(2)}, u32[]{:S(2)}) %collective-permute-start.35) | collective-permute-done | bytes 393248 | tf_op jit(solution)/shard_map/ppermute | solution.py:21
  226.6 5.0 %collective-permute-done.58 = bf16[192,768]{1,0:T(8,128)(2,1)S(1)} collective-permute-done((bf16[192,768]{1,0:T(8,128)(2,1)}, bf16[192,768]{1,0:T(8,128)(2,1)S(1)}, u32[]{:S(2)}, u32[]{:S(2)}) %collective-permute-start.58) | collective-permute-done | bytes 294944 | tf_op jit(solution)/shard_map/ppermute | solution.py:21
  237.8 2.7 collective-permute-done.42
  252.1 3.0 collective-permute-start.59
  259.7 5.1 %collective-permute-done.48 = bf16[192,576]{1,0:T(8,128)(2,1)S(1)} collective-permute-done((bf16[192,576]{1,0:T(8,128)(2,1)}, bf16[192,576]{1,0:T(8,128)(2,1)S(1)}, u32[]{:S(2)}, u32[]{:S(2)}) %collective-permute-start.48) | collective-permute-done | bytes 221216 | tf_op jit(solution)/shard_map/ppermute | solution.py:21
  267.0 7.5 %collective-permute-done.27 = bf16[2,128,768]{2,1,0:T(8,128)(2,1)} collective-permute-done((bf16[2,128,768]{2,1,0:T(8,128)(2,1)}, bf16[2,128,768]{2,1,0:T(8,128)(2,1)}, u32[]{:S(2)}, u32[]{:S(2)}) %collective-permute-start.27) | collective-permute-done | bytes 393248 | tf_op jit(solution)/shard_map/ppermute | solution.py:21
  275.2 5.9 %collective-permute-done.59 = bf16[192,768]{1,0:T(8,128)(2,1)} collective-permute-done((bf16[192,768]{1,0:T(8,128)(2,1)}, bf16[192,768]{1,0:T(8,128)(2,1)}, u32[]{:S(2)}, u32[]{:S(2)}) %collective-permute-start.59) | collective-permute-done | bytes 294944 | tf_op jit(solution)/shard_map/ppermute | solution.py:21
  291.3 5.7 %collective-permute-done.49 = bf16[192,576]{1,0:T(8,128)(2,1)S(1)} collective-permute-done((bf16[192,576]{1,0:T(8,128)(2,1)S(1)}, bf16[192,576]{1,0:T(8,128)(2,1)S(1)}, u32[]{:S(2)}, u32[]{:S(2)}) %collective-permute-start.49) | collective-permute-done | bytes 221216 | tf_op jit(solution)/shard_map/ppermute | solution.py:21
  299.2 11.7 %collective-permute-done.28 = bf16[2,128,768]{2,1,0:T(8,128)(2,1)S(1)} collective-permute-done((bf16[2,128,768]{2,1,0:T(8,128)(2,1)}, bf16[2,128,768]{2,1,0:T(8,128)(2,1)S(1)}, u32[]{:S(2)}, u32[]{:S(2)}) %collective-permute-start.28) | collective-permute-done | bytes 393248 | tf_op jit(solution)/shard_map/ppermute | solution.py:21
  314.6 3.4 %collective-permute-done.52 = bf16[192,384]{1,0:T(8,128)(2,1)} collective-permute-done((bf16[192,384]{1,0:T(8,128)(2,1)S(1)}, bf16[192,384]{1,0:T(8,128)(2,1)}, u32[]{:S(2)}, u32[]{:S(2)}) %collective-permute-start.52) | collective-permute-done | bytes 147488 | tf_op jit(solution)/shard_map/ppermute | solution.py:21
  (409 shorter events, 153.0 us)
Async XLA Ops:
  6.5 30.4 %collective-permute-start.2 = (bf16[584,192]{1,0:T(8,128)(2,1)}, bf16[584,192]{1,0:T(8,128)(2,1)}, u32[]{:S(2)}, u32[]{:S(2)}) collective-permute-start(bf16[584,192]{1,0:T(8,128)(2,1)} %pad_maximum_fusion.16), channel_id=1, source_target_pairs={{0,16},{8,24},{16,0},{24,8},{1,17},{9,25},{17,1},{25,9},{2,18},{10... | collective-permute-start | bytes 672776 | tf_op jit(solution)/shard_map/ppermute | solution.py:21
  9.5 32.1 %collective-permute-start.4 = (bf16[584,192]{1,0:T(8,128)(2,1)}, bf16[584,192]{1,0:T(8,128)(2,1)}, u32[]{:S(2)}, u32[]{:S(2)}) collective-permute-start(bf16[584,192]{1,0:T(8,128)(2,1)} %pad_maximum_fusion.16), channel_id=1, source_target_pairs={{0,8},{8,0},{16,24},{24,16},{1,9},{9,1},{17,25},{25,17},{2,10},{10... | collective-permute-start | bytes 672776 | tf_op jit(solution)/shard_map/ppermute | solution.py:21
  14.1 22.9 %collective-permute-start.1 = (bf16[257,768]{1,0:T(8,128)(2,1)S(1)}, bf16[257,768]{1,0:T(8,128)(2,1)}, u32[]{:S(2)}, u32[]{:S(2)}) collective-permute-start(bf16[257,768]{1,0:T(8,128)(2,1)S(1)} %pad_maximum_fusion.11), channel_id=1, source_target_pairs={{0,4},{4,0},{1,5},{5,1},{2,6},{6,2},{3,7},{7,3},{8,12},{12,8},{9,1... | collective-permute-start | bytes 1184264 | tf_op jit(solution)/shard_map/ppermute | solution.py:21
  23.8 63.6 %collective-permute-start.14 = (bf16[384,768]{1,0:T(8,128)(2,1)}, bf16[384,768]{1,0:T(8,128)(2,1)}, u32[]{:S(2)}, u32[]{:S(2)}) collective-permute-start(bf16[384,768]{1,0:T(8,128)(2,1)} %pad_maximum_fusion.10), channel_id=1, source_target_pairs={{0,16},{8,24},{16,0},{24,8},{1,17},{9,25},{17,1},{25,9},{2,18},{10... | collective-permute-start | bytes 1769480 | tf_op jit(solution)/shard_map/ppermute | solution.py:21
  36.1 71.3 %collective-permute-start.16 = (bf16[384,768]{1,0:T(8,128)(2,1)}, bf16[384,768]{1,0:T(8,128)(2,1)}, u32[]{:S(2)}, u32[]{:S(2)}) collective-permute-start(bf16[384,768]{1,0:T(8,128)(2,1)} %pad_maximum_fusion.10), channel_id=1, source_target_pairs={{0,8},{8,0},{16,24},{24,16},{1,9},{9,1},{17,25},{25,17},{2,10},{10... | collective-permute-start | bytes 1769480 | tf_op jit(solution)/shard_map/ppermute | solution.py:21
  36.9 27.3 %collective-permute-start.17 = (bf16[384,768]{1,0:T(8,128)(2,1)}, bf16[384,768]{1,0:T(8,128)(2,1)}, u32[]{:S(2)}, u32[]{:S(2)}) collective-permute-start(bf16[384,768]{1,0:T(8,128)(2,1)} %pad_maximum_fusion.10), channel_id=1, source_target_pairs={{0,2},{1,3},{2,0},{3,1},{4,6},{5,7},{6,4},{7,5},{8,10},{9,11},{10,... | collective-permute-start | bytes 1769480 | tf_op jit(solution)/shard_map/ppermute | solution.py:21
  41.6 22.7 %collective-permute-start = (bf16[512,768]{1,0:T(8,128)(2,1)S(1)}, bf16[512,768]{1,0:T(8,128)(2,1)}, u32[]{:S(2)}, u32[]{:S(2)}) collective-permute-start(bf16[512,768]{1,0:T(8,128)(2,1)S(1)} %dynamic-slice_bitcast_fusion), channel_id=1, source_target_pairs={{0,4},{4,0},{1,5},{5,1},{2,6},{6,2},{3,7},{7,3},{8,12},{12,8},{9,1... | collective-permute-start | bytes 2359304 | tf_op jit(solution)/shard_map/ppermute | solution.py:21
  53.2 34.0 %collective-permute-start.12 = (bf16[192,768]{0,1:T(8,128)(2,1)}, bf16[192,768]{0,1:T(8,128)(2,1)}, u32[]{:S(2)}, u32[]{:S(2)}) collective-permute-start(bf16[192,768]{0,1:T(8,128)(2,1)} %pad_maximum_fusion.12), channel_id=1, source_target_pairs={{0,8},{8,0},{16,24},{24,16},{1,9},{9,1},{17,25},{25,17},{2,10},{10... | collective-permute-start | bytes 884744 | tf_op jit(solution)/shard_map/ppermute | solution.py:21
  64.2 23.6 %collective-permute-start.11 = (bf16[192,768]{0,1:T(8,128)(2,1)}, bf16[192,768]{0,1:T(8,128)(2,1)}, u32[]{:S(2)}, u32[]{:S(2)}) collective-permute-start(bf16[192,768]{0,1:T(8,128)(2,1)} %collective-permute-done.10), channel_id=1, source_target_pairs={{0,8},{8,0},{16,24},{24,16},{1,9},{9,1},{17,25},{25,17},{2,10},{10... | collective-permute-start | bytes 884744 | tf_op jit(solution)/shard_map/ppermute | solution.py:21
  64.2 45.5 %collective-permute-start.18 = (bf16[384,768]{1,0:T(8,128)(2,1)}, bf16[384,768]{1,0:T(8,128)(2,1)}, u32[]{:S(2)}, u32[]{:S(2)}) collective-permute-start(bf16[384,768]{1,0:T(8,128)(2,1)} %collective-permute-done.17), channel_id=1, source_target_pairs={{0,16},{8,24},{16,0},{24,8},{1,17},{9,25},{17,1},{25,9},{2,18},{10... | collective-permute-start | bytes 1769480 | tf_op jit(solution)/shard_map/ppermute | solution.py:21
  87.1 37.0 %collective-permute-start.20 = (bf16[384,768]{1,0:T(8,128)(2,1)}, bf16[384,768]{1,0:T(8,128)(2,1)S(1)}, u32[]{:S(2)}, u32[]{:S(2)}) collective-permute-start(bf16[384,768]{1,0:T(8,128)(2,1)} %collective-permute-done.17), channel_id=1, source_target_pairs={{0,8},{8,0},{16,24},{24,16},{1,9},{9,1},{17,25},{25,17},{2,10},{10... | collective-permute-start | bytes 1769480 | tf_op jit(solution)/shard_map/ppermute | solution.py:21
  87.4 20.0 %collective-permute-start.15 = (bf16[384,768]{1,0:T(8,128)(2,1)}, bf16[384,768]{1,0:T(8,128)(2,1)S(1)}, u32[]{:S(2)}, u32[]{:S(2)}) collective-permute-start(bf16[384,768]{1,0:T(8,128)(2,1)} %collective-permute-done.14), channel_id=1, source_target_pairs={{0,8},{8,0},{16,24},{24,16},{1,9},{9,1},{17,25},{25,17},{2,10},{10... | collective-permute-start | bytes 1769480 | tf_op jit(solution)/shard_map/ppermute | solution.py:21
  121.5 26.3 %collective-permute-start.55 = (bf16[2,192,768]{2,1,0:T(8,128)(2,1)S(1)}, bf16[2,192,768]{2,1,0:T(8,128)(2,1)S(1)}, u32[]{:S(2)}, u32[]{:S(2)}) collective-permute-start(bf16[2,192,768]{2,1,0:T(8,128)(2,1)S(1)} %dynamic-slice_bitcast_fusion.4), channel_id=1, source_target_pairs={{0,8},{8,0},{16,24},{24,16},{1,9},{9,1},{17,25},{25,17},{2,10},{10... | collective-permute-start | bytes 1769480 | tf_op jit(solution)/shard_map/ppermute | solution.py:21
  121.7 27.6 %collective-permute-start.61 = (bf16[2,192,768]{2,1,0:T(8,128)(2,1)S(1)}, bf16[2,192,768]{2,1,0:T(8,128)(2,1)S(1)}, u32[]{:S(2)}, u32[]{:S(2)}) collective-permute-start(bf16[2,192,768]{2,1,0:T(8,128)(2,1)S(1)} %dynamic-slice_bitcast_fusion.2), channel_id=1, source_target_pairs={{0,8},{8,0},{16,24},{24,16},{1,9},{9,1},{17,25},{25,17},{2,10},{10... | collective-permute-start | bytes 1769480 | tf_op jit(solution)/shard_map/ppermute | solution.py:21
  130.5 19.7 %collective-permute-start.30 = (bf16[256,768]{1,0:T(8,128)(2,1)S(1)}, bf16[256,768]{1,0:T(8,128)(2,1)S(1)}, u32[]{:S(2)}, u32[]{:S(2)}) collective-permute-start(bf16[256,768]{1,0:T(8,128)(2,1)S(1)} %slice.371), channel_id=1, source_target_pairs={{0,1},{1,0},{2,3},{3,2},{4,5},{5,4},{6,7},{7,6},{8,9},{9,8},{10,11... | collective-permute-start | bytes 1179656 | tf_op jit(solution)/shard_map/ppermute | solution.py:21
  147.9 46.2 %collective-permute-start.57 = (bf16[2,192,768]{2,1,0:T(8,128)(2,1)}, bf16[2,192,768]{2,1,0:T(8,128)(2,1)}, u32[]{:S(2)}, u32[]{:S(2)}) collective-permute-start(bf16[2,192,768]{2,1,0:T(8,128)(2,1)} %dynamic-slice_bitcast_fusion.3), channel_id=1, source_target_pairs={{0,8},{8,0},{16,24},{24,16},{1,9},{9,1},{17,25},{25,17},{2,10},{10... | collective-permute-start | bytes 1769480 | tf_op jit(solution)/shard_map/ppermute | solution.py:21
  147.9 48.0 %collective-permute-start.63 = (bf16[2,192,768]{2,1,0:T(8,128)(2,1)}, bf16[2,192,768]{2,1,0:T(8,128)(2,1)}, u32[]{:S(2)}, u32[]{:S(2)}) collective-permute-start(bf16[2,192,768]{2,1,0:T(8,128)(2,1)} %dynamic-slice_bitcast_fusion.1), channel_id=1, source_target_pairs={{0,8},{8,0},{16,24},{24,16},{1,9},{9,1},{17,25},{25,17},{2,10},{10... | collective-permute-start | bytes 1769480 | tf_op jit(solution)/shard_map/ppermute | solution.py:21
  160.8 104.3 %collective-permute-start.56 = (bf16[192,768]{1,0:T(8,128)(2,1)}, bf16[192,768]{1,0:T(8,128)(2,1)}, u32[]{:S(2)}, u32[]{:S(2)}) collective-permute-start(bf16[192,768]{1,0:T(8,128)(2,1)} %fusion.38), channel_id=1, source_target_pairs={{0,16},{8,24},{16,0},{24,8},{1,17},{9,25},{17,1},{25,9},{2,18},{10... | collective-permute-start | bytes 884744 | tf_op jit(solution)/shard_map/ppermute | solution.py:21
  165.5 33.9 %collective-permute-start.26 = (bf16[128,768]{1,0:T(8,128)(2,1)}, bf16[128,768]{1,0:T(8,128)(2,1)}, u32[]{:S(2)}, u32[]{:S(2)}) collective-permute-start(bf16[128,768]{1,0:T(8,128)(2,1)} %dynamic-slice_bitcast_fusion.9), channel_id=1, source_target_pairs={{0,4},{4,0},{1,5},{5,1},{2,6},{6,2},{3,7},{7,3},{8,12},{12,8},{9,1... | collective-permute-start | bytes 589832 | tf_op jit(solution)/shard_map/ppermute | solution.py:21
  194.0 27.5 %collective-permute-start.35 = (bf16[2,128,768]{2,1,0:T(8,128)(2,1)}, bf16[2,128,768]{2,1,0:T(8,128)(2,1)S(1)}, u32[]{:S(2)}, u32[]{:S(2)}) collective-permute-start(bf16[2,128,768]{2,1,0:T(8,128)(2,1)} %get-tuple-element.79), channel_id=1, source_target_pairs={{0,2},{1,3},{2,0},{3,1},{4,6},{5,7},{6,4},{7,5},{8,10},{9,11},{10,... | collective-permute-start | bytes 1179656 | tf_op jit(solution)/shard_map/ppermute | solution.py:21
  195.9 26.2 %collective-permute-start.34 = (bf16[2,128,768]{2,1,0:T(8,128)(2,1)}, bf16[2,128,768]{2,1,0:T(8,128)(2,1)S(1)}, u32[]{:S(2)}, u32[]{:S(2)}) collective-permute-start(bf16[2,128,768]{2,1,0:T(8,128)(2,1)} %get-tuple-element.77), channel_id=1, source_target_pairs={{0,1},{1,0},{2,3},{3,2},{4,5},{5,4},{6,7},{7,6},{8,9},{9,8},{10,11... | collective-permute-start | bytes 1179656 | tf_op jit(solution)/shard_map/ppermute | solution.py:21
  199.5 83.7 %collective-permute-start.62 = (bf16[192,768]{1,0:T(8,128)(2,1)}, bf16[192,768]{1,0:T(8,128)(2,1)}, u32[]{:S(2)}, u32[]{:S(2)}) collective-permute-start(bf16[192,768]{1,0:T(8,128)(2,1)} %fusion.31), channel_id=1, source_target_pairs={{0,16},{8,24},{16,0},{24,8},{1,17},{9,25},{17,1},{25,9},{2,18},{10... | collective-permute-start | bytes 884744 | tf_op jit(solution)/shard_map/ppermute | solution.py:21
  201.9 45.1 %collective-permute-start.50 = (bf16[2,192,768]{2,1,0:T(8,128)(2,1)}, bf16[2,192,768]{2,1,0:T(8,128)(2,1)}, u32[]{:S(2)}, u32[]{:S(2)}) collective-permute-start(bf16[2,192,768]{2,1,0:T(8,128)(2,1)} %dynamic-slice_bitcast_fusion.5), channel_id=1, source_target_pairs={{0,8},{8,0},{16,24},{24,16},{1,9},{9,1},{17,25},{25,17},{2,10},{10... | collective-permute-start | bytes 1769480 | tf_op jit(solution)/shard_map/ppermute | solution.py:21
  241.8 32.7 %collective-permute-start.27 = (bf16[2,128,768]{2,1,0:T(8,128)(2,1)}, bf16[2,128,768]{2,1,0:T(8,128)(2,1)}, u32[]{:S(2)}, u32[]{:S(2)}) collective-permute-start(bf16[2,128,768]{2,1,0:T(8,128)(2,1)} %pad_maximum_fusion.13), channel_id=1, source_target_pairs={{0,2},{1,3},{2,0},{3,1},{4,6},{5,7},{6,4},{7,5},{8,10},{9,11},{10,... | collective-permute-start | bytes 1179656 | tf_op jit(solution)/shard_map/ppermute | solution.py:21
  252.1 28.9 %collective-permute-start.59 = (bf16[192,768]{1,0:T(8,128)(2,1)}, bf16[192,768]{1,0:T(8,128)(2,1)}, u32[]{:S(2)}, u32[]{:S(2)}) collective-permute-start(bf16[192,768]{1,0:T(8,128)(2,1)} %fusion.37), channel_id=1, source_target_pairs={{0,2},{1,3},{2,0},{3,1},{4,6},{5,7},{6,4},{7,5},{8,10},{9,11},{10,... | collective-permute-start | bytes 884744 | tf_op jit(solution)/shard_map/ppermute | solution.py:21
  264.9 22.4 %collective-permute-start.65 = (bf16[192,768]{1,0:T(8,128)(2,1)}, bf16[192,768]{1,0:T(8,128)(2,1)S(1)}, u32[]{:S(2)}, u32[]{:S(2)}) collective-permute-start(bf16[192,768]{1,0:T(8,128)(2,1)} %fusion.30), channel_id=1, source_target_pairs={{0,2},{1,3},{2,0},{3,1},{4,6},{5,7},{6,4},{7,5},{8,10},{9,11},{10,... | collective-permute-start | bytes 884744 | tf_op jit(solution)/shard_map/ppermute | solution.py:21
  265.1 33.1 %collective-permute-start.29 = (bf16[2,128,768]{2,1,0:T(8,128)(2,1)}, bf16[2,128,768]{2,1,0:T(8,128)(2,1)S(1)}, u32[]{:S(2)}, u32[]{:S(2)}) collective-permute-start(bf16[2,128,768]{2,1,0:T(8,128)(2,1)} %pad_maximum_fusion.13), channel_id=1, source_target_pairs={{0,1},{1,0},{2,3},{3,2},{4,5},{5,4},{6,7},{7,6},{8,9},{9,8},{10,11... | collective-permute-start | bytes 1179656 | tf_op jit(solution)/shard_map/ppermute | solution.py:21
  281.1 29.8 %collective-permute-start.28 = (bf16[2,128,768]{2,1,0:T(8,128)(2,1)}, bf16[2,128,768]{2,1,0:T(8,128)(2,1)S(1)}, u32[]{:S(2)}, u32[]{:S(2)}) collective-permute-start(bf16[2,128,768]{2,1,0:T(8,128)(2,1)} %collective-permute-done.27), channel_id=1, source_target_pairs={{0,1},{1,0},{2,3},{3,2},{4,5},{5,4},{6,7},{7,6},{8,9},{9,8},{10,11... | collective-permute-start | bytes 1179656 | tf_op jit(solution)/shard_map/ppermute | solution.py:21
  283.2 37.9 %collective-permute-start.38 = (bf16[2,128,768]{2,1,0:T(8,128)(2,1)}, bf16[2,128,768]{2,1,0:T(8,128)(2,1)}, u32[]{:S(2)}, u32[]{:S(2)}) collective-permute-start(bf16[2,128,768]{2,1,0:T(8,128)(2,1)} %pad_maximum_fusion.15), channel_id=1, source_target_pairs={{0,2},{1,3},{2,0},{3,1},{4,6},{5,7},{6,4},{7,5},{8,10},{9,11},{10,... | collective-permute-start | bytes 1179656 | tf_op jit(solution)/shard_map/ppermute | solution.py:21
  287.3 42.8 %collective-permute-start.40 = (bf16[2,128,768]{2,1,0:T(8,128)(2,1)}, bf16[2,128,768]{2,1,0:T(8,128)(2,1)}, u32[]{:S(2)}, u32[]{:S(2)}) collective-permute-start(bf16[2,128,768]{2,1,0:T(8,128)(2,1)} %pad_maximum_fusion.15), channel_id=1, source_target_pairs={{0,1},{1,0},{2,3},{3,2},{4,5},{5,4},{6,7},{7,6},{8,9},{9,8},{10,11... | collective-permute-start | bytes 1179656 | tf_op jit(solution)/shard_map/ppermute | solution.py:21
  297.0 22.1 %collective-permute-start.60 = (bf16[192,768]{1,0:T(8,128)(2,1)}, bf16[192,768]{1,0:T(8,128)(2,1)}, u32[]{:S(2)}, u32[]{:S(2)}) collective-permute-start(bf16[192,768]{1,0:T(8,128)(2,1)} %fusion.41), channel_id=1, source_target_pairs={{0,4},{4,0},{1,5},{5,1},{2,6},{6,2},{3,7},{7,3},{8,12},{12,8},{9,1... | collective-permute-start | bytes 884744 | tf_op jit(solution)/shard_map/ppermute | solution.py:21
  298.1 27.5 %collective-permute-start.66 = (bf16[192,768]{1,0:T(8,128)(2,1)}, bf16[192,768]{1,0:T(8,128)(2,1)}, u32[]{:S(2)}, u32[]{:S(2)}) collective-permute-start(bf16[192,768]{1,0:T(8,128)(2,1)} %fusion.34), channel_id=1, source_target_pairs={{0,4},{4,0},{1,5},{5,1},{2,6},{6,2},{3,7},{7,3},{8,12},{12,8},{9,1... | collective-permute-start | bytes 884744 | tf_op jit(solution)/shard_map/ppermute | solution.py:21
  (81 other events, 697.2 us)
